TPU v7x, 32 devices: a whole 2x2x4 slice. The times are simulated.
32 devices in a mesh: chars: 2 (over x), prow: 16 (over z, y, core).
Axes of the slice: x: 2, y: 2, z: 4, core: 2. Of those that a mesh axis runs over, the one named last changes fastest.
Arguments:
- queries: bfloat16 [8192, 512], P(('chars', 'prow')), parts along dimension 0, may hold values from -8 to 8
- keys: bfloat16 [8192, 512], P(('chars', 'prow')), parts along dimension 0, may hold values from -8 to 8
- values: bfloat16 [8192, 512], P(('chars', 'prow')), parts along dimension 0, may hold values from -6 to 6
- out_grad: bfloat16 [8192, 512], P(('chars', 'prow')), parts along dimension 0, may hold values from -6 to 6
- valid_counts: int32 [32, 4], P('chars'), parts along dimension 0, may hold values from 1 to 64
- landmark_cols: int32 [32], P('chars'), parts along dimension 0, may hold values from 0 to 3
- landmark_rows: int32 [32, 4], P(('chars', 'prow')), parts along dimension 0, may hold values from 0 to 15, as said below
Outputs:
- attn_out: bfloat16 [8192, 512], P(('chars', 'prow')), parts along dimension 0
- query_grad: bfloat16 [8192, 512], P(('chars', 'prow')), parts along dimension 0
- key_grad: bfloat16 [8192, 512], P(('chars', 'prow')), parts along dimension 0
- value_grad: bfloat16 [8192, 512], P(('chars', 'prow')), parts along dimension 0
There are 2 independent parts, one for each index of `chars`. A program takes and returns all parts, laid end to end along the dimension named above; each array names one. Nothing has to cross between parts.
Inputs may be any that keep to these rules, and one draw needn't show every extreme that they name: `landmark_rows`: the 4 entries of each row are distinct.
All inputs are finite; a program needn't handle non-finite values.
Results may differ from a plain program's by a relative error of at most 0.012.
The roundings to bfloat16 on the way count: a program that leaves them out, or rounds other values in their place, can miss the bound.
Values may be sent and summed in bfloat16 or wider, within the bound.
A program may use at most 192 MiB of HBM per device.

v0:
```python
import math
import jax
import jax.numpy as jnp
from jax import lax
from jax.sharding import PartitionSpec as P

HEADS = 8
HD = 64
BLK = 64
NLAND = 4
PC = 4
masked_score = -1e30


def extended(x, sides, width):
    for axis, dim in sides:
        devices, length = (lax.axis_size(axis), x.shape[dim])
        up = [(i, (i + 1) % devices) for i in range(devices - 1)]
        down = [(j, i) for i, j in up]
        last = lax.slice_in_dim(x, length - width, length, axis=dim)
        first = lax.slice_in_dim(x, 0, width, axis=dim)
        before = lax.ppermute(last, axis, up)
        after = lax.ppermute(first, axis, down)
        x = jnp.concatenate([before, x, after], axis=dim)
    return x


def passed_along(block, axis, distance):
    devices = range(lax.axis_size(axis))
    route = [(i - distance, i) for i in devices if i - distance in devices]
    return lax.ppermute(block, axis, route)


def product(form, left, right):
    return jnp.einsum(form, left, right, preferred_element_type=jnp.float32)


def window_stack(near_rows, columns):
    pieces = [
        near_rows[row_off, col_off : col_off + columns]
        for row_off in range(3)
        for col_off in range(3)
    ]
    stacked = jnp.stack(pieces, axis=1)
    return stacked.reshape(columns, 9 * stacked.shape[2], stacked.shape[3])


def window_mask(count_near, columns, block_len):
    pieces = [
        count_near[row_off, col_off : col_off + columns]
        for row_off in range(3)
        for col_off in range(3)
    ]
    counts = jnp.stack(pieces, axis=1)
    position = jnp.arange(block_len)
    return (position[None, None, :] < counts[:, :, None]).reshape(columns, 9 * block_len)


def spread(grad_window, columns, block_len):
    pieces = grad_window.reshape(columns, 9, block_len, grad_window.shape[-1])
    layers = []
    for row_off in range(3):
        left = jnp.pad(pieces[:, row_off * 3], ((0, 2), (0, 0), (0, 0)))
        middle = jnp.pad(pieces[:, row_off * 3 + 1], ((1, 1), (0, 0), (0, 0)))
        right = jnp.pad(pieces[:, row_off * 3 + 2], ((2, 0), (0, 0), (0, 0)))
        layers.append(left + middle + right)
    return jnp.stack(layers)


def attend(
    query_blocks,
    grad_raw,
    keys_win,
    values_win,
    mask_win,
    keys_land,
    values_land,
    mask_land,
    query_valid,
):
    score_scale = 1.0 / math.sqrt(query_blocks.shape[-1])
    scores_win = product("cqhe,cwhe->chqw", query_blocks, keys_win) * score_scale
    scores_land = product("cqhe,lhe->chql", query_blocks, keys_land) * score_scale
    scores_win = jnp.where(mask_win[:, None, None, :], scores_win, masked_score)
    scores_land = jnp.where(mask_land[None, None, None, :], scores_land, masked_score)
    row_max = jnp.maximum(jnp.max(scores_win, axis=-1), jnp.max(scores_land, axis=-1))
    exp_total = jnp.sum(jnp.exp(scores_win - row_max[..., None]), axis=-1) + jnp.sum(
        jnp.exp(scores_land - row_max[..., None]), axis=-1
    )
    log_total = row_max + jnp.log(exp_total)
    probs_win = jnp.exp(scores_win - log_total[..., None])
    probs_land = jnp.exp(scores_land - log_total[..., None])
    low_win = probs_win.astype(jnp.bfloat16)
    low_land = probs_land.astype(jnp.bfloat16)
    mixed_out = product("chqw,cwhe->cqhe", low_win, values_win) + product(
        "chql,lhe->cqhe", low_land, values_land
    )
    query_mask = query_valid[:, :, None, None]
    attn_part = jnp.where(query_mask, mixed_out, 0.0).astype(jnp.bfloat16)
    grad_in = jnp.where(query_mask, grad_raw, jnp.zeros_like(grad_raw))
    row_delta = jnp.sum(grad_in.astype(jnp.float32) * mixed_out, axis=-1)
    row_delta = jnp.transpose(row_delta, (0, 2, 1))[..., None]
    dprob_win = product("cqhe,cwhe->chqw", grad_in, values_win)
    dprob_land = product("cqhe,lhe->chql", grad_in, values_land)
    dscore_win = (probs_win * (dprob_win - row_delta) * score_scale).astype(jnp.bfloat16)
    dscore_land = (probs_land * (dprob_land - row_delta) * score_scale).astype(jnp.bfloat16)
    query_part = (
        product("chqw,cwhe->cqhe", dscore_win, keys_win)
        + product("chql,lhe->cqhe", dscore_land, keys_land)
    ).astype(jnp.bfloat16)
    kgrad_win = product("chqw,cqhe->cwhe", dscore_win, query_blocks)
    vgrad_win = product("chqw,cqhe->cwhe", low_win, grad_in)
    kgrad_land = product("chql,cqhe->lhe", dscore_land, query_blocks)
    vgrad_land = product("chql,cqhe->lhe", low_land, grad_in)
    return (attn_part, query_part, kgrad_win, vgrad_win, kgrad_land, vgrad_land)


def per_device(queries, keys, values, out_grad, valid_counts, landmark_cols, landmark_rows):
    model_width = HEADS * HD
    my_row = lax.axis_index("prow")
    row_total = lax.axis_size("prow")
    position = jnp.arange(BLK)
    key_value = jnp.concatenate([keys, values], axis=1).reshape(1, PC, BLK, 2 * model_width)
    near_rows = extended(key_value, (("prow", 0),), 1)
    near_rows = jnp.pad(near_rows, ((0, 0), (1, 1), (0, 0), (0, 0)))
    count_padded = jnp.pad(valid_counts, ((1, 1), (1, 1)))
    count_near = lax.dynamic_slice_in_dim(count_padded, my_row, 3, 0)
    own_col = lax.dynamic_index_in_dim(landmark_cols, my_row, 0, keepdims=False)
    own_block = lax.dynamic_slice_in_dim(key_value[0], own_col, 1, 0)
    land_panel = lax.all_gather(own_block, "prow", axis=0, tiled=True)
    chosen_rows = landmark_rows[0]
    chosen = jnp.take(land_panel, chosen_rows, axis=0)
    chosen_counts = valid_counts[chosen_rows, landmark_cols[chosen_rows]]
    stacked = window_stack(near_rows, PC)
    keys_win = stacked[..., :model_width].reshape(PC, 9 * BLK, HEADS, HD)
    values_win = stacked[..., model_width:].reshape(PC, 9 * BLK, HEADS, HD)
    mask_win = window_mask(count_near, PC, BLK)
    keys_land = chosen[..., :model_width].reshape(NLAND * BLK, HEADS, HD)
    values_land = chosen[..., model_width:].reshape(NLAND * BLK, HEADS, HD)
    mask_land = (position[None, :] < chosen_counts[:, None]).reshape(NLAND * BLK)
    row_counts = lax.dynamic_index_in_dim(valid_counts, my_row, 0, keepdims=False)
    query_valid = position[None, :] < row_counts[:, None]
    attn_part, query_part, kgrad_win, vgrad_win, kgrad_land, vgrad_land = attend(
        queries.reshape(PC, BLK, HEADS, HD),
        out_grad.reshape(PC, BLK, HEADS, HD),
        keys_win,
        values_win,
        mask_win,
        keys_land,
        values_land,
        mask_land,
        query_valid,
    )
    grad_window = jnp.concatenate(
        [kgrad_win.reshape(PC, 9 * BLK, model_width), vgrad_win.reshape(PC, 9 * BLK, model_width)],
        axis=-1,
    )
    summed = spread(grad_window, PC, BLK)
    own_grads = summed[1, 1 : PC + 1]
    from_above = passed_along(summed[2, 1 : PC + 1], "prow", 1)
    from_below = passed_along(summed[0, 1 : PC + 1], "prow", -1)
    grad_land = jnp.concatenate(
        [kgrad_land.reshape(NLAND, BLK, model_width), vgrad_land.reshape(NLAND, BLK, model_width)],
        axis=-1,
    )
    slot_grads = (
        jnp.zeros((row_total, BLK, 2 * model_width), jnp.float32).at[chosen_rows].add(grad_land)
    )
    land_total = lax.psum_scatter(slot_grads, "prow", scatter_dimension=0, tiled=True)[0]
    hit_mask = (jnp.arange(PC) == own_col)[:, None, None]
    all_grads = own_grads + from_above + from_below + jnp.where(hit_mask, land_total[None], 0.0)
    attn_out = attn_part.reshape(PC * BLK, model_width)
    query_grad = query_part.reshape(PC * BLK, model_width)
    key_grad = all_grads[..., :model_width].astype(jnp.bfloat16).reshape(PC * BLK, model_width)
    value_grad = all_grads[..., model_width:].astype(jnp.bfloat16).reshape(PC * BLK, model_width)
    return (attn_out, query_grad, key_grad, value_grad)


def solution(mesh):
    return jax.shard_map(
        per_device,
        mesh=mesh,
        in_specs=(
            P(("chars", "prow"), None),
            P(("chars", "prow"), None),
            P(("chars", "prow"), None),
            P(("chars", "prow"), None),
            P("chars", None),
            P("chars"),
            P(("chars", "prow"), None),
        ),
        out_specs=(
            P(("chars", "prow"), None),
            P(("chars", "prow"), None),
            P(("chars", "prow"), None),
            P(("chars", "prow"), None),
        ),
        check_vma=False,
    )
```

profile of v0, /device:TPU:1, one launch (start us, length us, event | category | flops | bytes accessed | tf_op | source)
XLA Modules:
  0.0 191.7 jit_solution(16934145135606755180)
XLA Ops:
  7.2 1.0 constant_dynamic-update-slice_fusion.1
  8.2 1.0 constant_dynamic-update-slice_fusion
  9.3 2.0 %collective-permute-start.1 = (bf16[1,4,64,1024]{3,2,1,0:T(8,128)(2,1)S(1)}, bf16[1,4,64,1024]{3,2,1,0:T(8,128)(2,1)S(1)}, u32[]{:S(2)}, u32[]{:S(2)}) collective-permute-start(bf16[1,4,64,1024]{3,2,1,0:T(8,128)(2,1)S(1)} %bitcast.260), channel_id=1, source_target_pairs={{1,0},{2,1},{3,2},{4,3},{5,4},{6,5},{7,6},{8,7},{9,8},{10,9},{11,1... | collective-permute-start | bytes 1572872 | tf_op jit(solution)/shard_map/ppermute | solution.py:23
  11.2 4.5 %collective-permute-start = (bf16[1,4,64,1024]{3,2,1,0:T(8,128)(2,1)S(1)}, bf16[1,4,64,1024]{3,2,1,0:T(8,128)(2,1)S(1)}, u32[]{:S(2)}, u32[]{:S(2)}) collective-permute-start(bf16[1,4,64,1024]{3,2,1,0:T(8,128)(2,1)S(1)} %bitcast.261), channel_id=1, source_target_pairs={{0,1},{1,2},{2,3},{3,4},{4,5},{5,6},{6,7},{7,8},{8,9},{9,10},{10,1... | collective-permute-start | bytes 1572872 | tf_op jit(solution)/shard_map/ppermute | solution.py:22
  15.7 1.2 dynamic_slice.16
  21.0 1.3 gather_fusion
  23.7 1.3 gather_fusion.1
  28.4 1.1 copy.153
  30.4 1.9 %fusion.46 = (bf16[4,576,512]{2,1,0:T(8,128)(2,1)S(1)}, bf16[4,576,512]{2,1,0:T(8,128)(2,1)}) fusion(bf16[4,576,1024]{2,1,0:T(8,128)(2,1)S(1)} %bitcast.259), kind=kLoop, calls=%fused_computation.124 | loop fusion | bytes 9437184 | tf_op jit(solution)/shard_map/slice | solution.py:136
  32.3 2.6 %copy.132 = bf16[4,576,512]{1,2,0:T(8,128)(2,1)} copy(bf16[4,576,512]{2,1,0:T(8,128)(2,1)S(1)} %get-tuple-element.15) | data formatting | bytes 4718592 | tf_op jit(solution)/shard_map/slice | solution.py:136
  34.8 3.1 %copy.142 = bf16[4,576,512]{1,2,0:T(8,128)(2,1)S(1)} copy(bf16[4,576,512]{2,1,0:T(8,128)(2,1)} %get-tuple-element.16) | data formatting | bytes 4718592 | tf_op jit(solution)/shard_map/slice | solution.py:135
  38.0 3.3 %bitcast_reduce_fusion = (f32[4,8,64]{2,1,0:T(8,128)S(1)}, f32[4,8,576,64]{2,3,1,0:T(8,128)}) fusion(pred[4,576]{1,0:T(4,128)(4,1)S(1)} %broadcast_compare_fusion, bf16[4,64,8,64]{1,3,2,0:T(8,128)(2,1)S(1)} %copy.161, bf16[4,576,8,64]{1,3,2,0:T(8,128)(2,1)S(1)} %bitcast.256), kind=kOutput, calls=%fused_computation.8 | convolution fusion | flops 154531840 | bytes 7350528 | tf_op jit(solution)/shard_map/cqhe,cwhe->chqw/dot_general | solution.py:35
  41.3 20.8 %all-gather.2.cloned.1.call-done = bf16[16,64,1024]{2,1,0:T(8,128)(2,1)} async-done(((bf16[1,64,1024]{2,1,0:T(8,128)(2,1)}), bf16[16,64,1024]{2,1,0:T(8,128)(2,1)}) %all-gather.2.cloned.1.call-update) | async-done | bytes 2097168 | tf_op jit(solution)/shard_map/all_gather | solution.py:130
  62.1 2.2 %gather_fusion.2 = bf16[4,64,1024]{2,1,0:T(8,128)(2,1)S(1)} fusion(bf16[16,64,1024]{2,1,0:T(8,128)(2,1)} %all-gather.2.cloned.1.call-done, s32[1024]{0:T(1024)S(1)} %pad_clamp_fusion), kind=kCustom, calls=%fused_computation.2 | custom fusion | bytes 1048592 | tf_op jit(solution)/shard_map/jit(_take)/gather | solution.py:132
  64.7 1.0 copy.150
  68.9 1.4 fusion.1
  72.0 2.4 %select_convert_fusion = (bf16[4,64,8,64]{1,3,2,0:T(8,128)(2,1)}, f32[4,64,8,64]{1,3,2,0:T(8,128)S(1)}) fusion(pred[4,64]{1,0:T(4,128)(4,1)S(1)} %iota_compare_fusion.3, f32[4,64,8,64]{1,3,2,0:T(8,128)S(1)} %convolution_bitcast_fusion.4, bf16[4,576,8,64]{1,3,2,0:T(8,128)(2,1)S(1)} %bitcast.266, f32[4,8,576,64]{2,3,1,0:T(8,128)S(1)} %copy-done, ...), kind=kOutput, calls=%fused_computation.63 | convolution fusion | flops 155975680 | bytes 8399360 | tf_op jit(solution)/shard_map/chqw,cwhe->cqhe/dot_general | solution.py:35
  74.6 1.1 copy.156
  75.7 1.5 convolution_bitcast_fusion.7
  77.2 2.5 %reshape.234 = f32[4,64,512]{1,0,2:T(4,128)} reshape(f32[256,8,64]{0,2,1:T(8,128)} %convolution_bitcast_fusion.7) | data formatting | bytes 1048576 | tf_op jit(solution)/shard_map/reshape | solution.py:163
  79.7 2.4 %copy.179 = f32[4,64,512]{2,1,0:T(8,128)} copy(f32[4,64,512]{1,0,2:T(4,128)} %reshape.234) | data formatting | bytes 1048576 | tf_op jit(solution)/shard_map/reshape | solution.py:163
  82.1 1.5 fusion.50
  84.4 1.0 copy-done.5
  86.7 2.5 %broadcast_in_dim.107 = f32[16,64,1024]{2,1,0:T(8,128)} broadcast(f32[]{:T(128)} %constant.32.clone.1), dimensions={} | broadcast | bytes 4194308 | tf_op jit(solution)/shard_map/broadcast_in_dim | solution.py:167
  89.2 3.1 %scatter_fusion = f32[16,64,1024]{2,1,0:T(8,128)} fusion(f32[16,64,1024]{2,1,0:T(8,128)} %broadcast_in_dim.107, s32[4]{0:T(128)S(1)} %fusion.44, f32[4,64,1024]{2,1,0:T(8,128)S(1)} %pad_maximum_fusion), kind=kCustom, calls=%fused_computation.3 | custom fusion | flops 262144 | bytes 3145744 | tf_op jit(solution)/shard_map/scatter-add | solution.py:167
  92.3 1.0 copy-done.9
  93.4 5.3 %multiply_convert_fusion = bf16[4,8,64,576]{3,2,1,0:T(8,128)(2,1)S(1)} fusion(f32[4,8,576,64]{2,3,1,0:T(8,128)} %get-tuple-element.31, f32[4,8,64]{2,1,0:T(8,128)S(1)} %bitcast.273, f32[4,8,64]{2,1,0:T(8,128)S(1)} %fusion.35, pred[4,576]{1,0:T(4,128)(4,1)S(1)} %broadcast_compare_fusion, bf16[4,64,8,64]{1,3,2,0:T(8,128)(2,1)S(1)} %copy-done.9, ...), kind=kOutput, calls=%fused_computation.12 | convolution fusion | flops 159252480 | bytes 9718016 | tf_op jit(solution)/shard_map/cqhe,cwhe->chqw/dot_general | solution.py:35
  98.7 1.5 copy-done.4
  100.1 3.1 %convolution_bitcast_fusion = f32[4,576,8,64]{1,3,2,0:T(8,128)} fusion(bf16[4,64,8,64]{1,3,2,0:T(8,128)(2,1)S(1)} %copy.161, bf16[4,8,64,576]{3,2,1,0:T(8,128)(2,1)S(1)} %multiply_convert_fusion), kind=kOutput, calls=%fused_computation.19 | convolution fusion | flops 150994944 | bytes 7340032 | tf_op jit(solution)/shard_map/chqw,cqhe->cwhe/dot_general | solution.py:35
  103.2 8.5 %copy.162 = f32[4,576,8,64]{3,2,1,0:T(8,128)} copy(f32[4,576,8,64]{1,3,2,0:T(8,128)} %convolution_bitcast_fusion) | data formatting | bytes 9437184 | tf_op jit(solution)/shard_map/chqw,cqhe->cwhe/transpose | solution.py:35
  111.7 9.0 %concatenate.23 = f32[4,9,64,512]{3,2,1,0:T(8,128)} reshape(f32[4,576,8,64]{3,2,1,0:T(8,128)} %copy.162) | data formatting | bytes 9437184 | tf_op jit(solution)/shard_map/concatenate | solution.py:154
  120.6 6.1 %convolution_bitcast_fusion.1 = f32[4,576,8,64]{1,3,2,0:T(8,128)} fusion(bf16[4,64,8,64]{1,3,2,0:T(8,128)(2,1)S(1)} %copy-done.9, f32[4,8,576,64]{2,3,1,0:T(8,128)} %get-tuple-element.31, f32[4,8,64]{2,1,0:T(8,128)S(1)} %fusion.35, pred[4,576]{1,0:T(4,128)(4,1)S(1)} %broadcast_compare_fusion), kind=kOutput, calls=%fused_computation.20 | convolution fusion | flops 155713536 | bytes 9709824 | tf_op jit(solution)/shard_map/chqw,cqhe->cwhe/dot_general | solution.py:35
  126.8 8.2 %copy.163 = f32[4,576,8,64]{3,2,1,0:T(8,128)} copy(f32[4,576,8,64]{1,3,2,0:T(8,128)} %convolution_bitcast_fusion.1) | data formatting | bytes 9437184 | tf_op jit(solution)/shard_map/chqw,cqhe->cwhe/transpose | solution.py:35
  135.0 9.0 %concatenate.24 = f32[4,9,64,512]{3,2,1,0:T(8,128)} reshape(f32[4,576,8,64]{3,2,1,0:T(8,128)} %copy.163) | data formatting | bytes 9437184 | tf_op jit(solution)/shard_map/concatenate | solution.py:154
  144.0 3.0 %constant_dynamic-update-slice_fusion.4 = f32[4,9,64,1024]{3,2,1,0:T(8,128)S(1)} fusion(f32[4,9,64,512]{3,2,1,0:T(8,128)} %concatenate.23), kind=kLoop, calls=%fused_computation.88 | loop fusion | bytes 9437184
  148.3 2.8 %slice_bitcast_fusion.11 = (f32[4,64,1024]{2,1,0:T(8,128)}, f32[4,64,1024]{2,1,0:T(8,128)S(1)}, f32[4,64,1024]{2,1,0:T(8,128)S(1)}, f32[4,64,1024]{2,1,0:T(8,128...) fusion(f32[4,9,64,1024]{3,2,1,0:T(8,128)S(1)} %constant_dynamic, ...), kind=kLoop, calls=%fused_computation.59 | loop fusion | bytes 18874368 | tf_op jit(solution)/shard_map/squeeze | solution.py:63
  151.4 1.1 slice_bitcast_fusion
  152.4 2.2 %collective-permute-start.3 = (f32[4,64,1024]{2,1,0:T(8,128)}, f32[4,64,1024]{2,1,0:T(8,128)}, u32[]{:S(2)}, u32[]{:S(2)}) collective-permute-start(f32[4,64,1024]{2,1,0:T(8,128)} %slice_bitcast_fusion), channel_id=1, source_target_pairs={{1,0},{2,1},{3,2},{4,3},{5,4},{6,5},{7,6},{8,7},{9,8},{10,9},{11,1... | collective-permute-start | bytes 3145736 | tf_op jit(solution)/shard_map/ppermute | solution.py:31
  154.9 1.1 slice_bitcast_fusion.4
  156.0 3.8 %collective-permute-start.2 = (f32[4,64,1024]{2,1,0:T(8,128)}, f32[4,64,1024]{2,1,0:T(8,128)}, u32[]{:S(2)}, u32[]{:S(2)}) collective-permute-start(f32[4,64,1024]{2,1,0:T(8,128)} %slice_bitcast_fusion.4), channel_id=1, source_target_pairs={{0,1},{1,2},{2,3},{3,4},{4,5},{5,6},{6,7},{7,8},{8,9},{9,10},{10,1... | collective-permute-start | bytes 3145736 | tf_op jit(solution)/shard_map/ppermute | solution.py:31
  160.5 1.4 copy.152
  161.8 1.0 reshape.188
  162.9 1.8 convolution_bitcast_fusion.2
  164.7 2.7 %fusion.16 = bf16[4,64,8,64]{1,3,2,0:T(8,128)(2,1)S(1)} fusion(f32[4,64,8,64]{1,3,2,0:T(8,128)S(1)} %convolution_bitcast_fusion.2, bf16[4,576,8,64]{1,3,2,0:T(8,128)(2,1)S(1)} %bitcast.257, bf16[4,8,64,576]{3,2,1,0:T(8,128)(2,1)} %copy-done.4), kind=kOutput, calls=%fused_computation.41 | convolution fusion | flops 151257088 | bytes 5505024 | tf_op jit(solution)/shard_map/chqw,cwhe->cqhe/dot_general | solution.py:35
  167.8 1.0 reshape.190
  168.8 2.1 %add_bitcast_fusion.2 = f32[1,6,64,1024]{3,2,1,0:T(8,128)S(1)} fusion(f32[4,64,1024]{2,1,0:T(8,128)} %get-tuple-element.11, f32[4,64,1024]{2,1,0:T(8,128)} %get-tuple-element.12, f32[4,64,1024]{2,1,0:T(8,128)} %get-tuple-element.6), kind=kLoop, calls=%fused_computation.34 | loop fusion | flops 786432 | bytes 4718592 | tf_op jit(solution)/shard_map/stack | solution.py:67
  171.0 11.1 %collective-permute-done.2 = f32[4,64,1024]{2,1,0:T(8,128)} collective-permute-done((f32[4,64,1024]{2,1,0:T(8,128)}, f32[4,64,1024]{2,1,0:T(8,128)}, u32[]{:S(2)}, u32[]{:S(2)}) %collective-permute-start.2) | collective-permute-done | bytes 1048608 | tf_op jit(solution)/shard_map/ppermute | solution.py:31
  182.1 2.0 %fusion.20 = bf16[4,64,1024]{2,1,0:T(8,128)(2,1)S(1)} fusion(f32[4,64,1024]{2,1,0:T(8,128)} %collective-permute-done.3, f32[4,64,1024]{2,1,0:T(8,128)} %collective-permute-done.2, f32[1,6,64,1024]{3,2,1,0:T(8,128)S(1)} %add_bitcast_fusion.2, f32[64,1024]{1,0:T(8,128)} %bitcast.269, pred[4]{0:T(512)(128)(4,1)S(1)} %iota_compare_fusion.4), kind=kLoop, calls=%fused_computation.56 | loop fusion | flops 1310720 | bytes 3932164 | tf_op jit(solution)/shard_map/convert.1
  (96 shorter events, 18.6 us)
Async XLA Ops:
  7.2 18.9 %copy-start.15 = (bf16[256,512]{1,0:T(8,128)(2,1)S(1)}, bf16[256,512]{1,0:T(8,128)(2,1)}, u32[]{:S(2)}) copy-start(bf16[256,512]{1,0:T(8,128)(2,1)} %param.7) | copy-start | bytes 786436
  7.2 54.9 %all-gather.2.cloned.1.call-start = ((), (), s32[]{:S(2)}) async-start(), calls=%async_computation.1 | async-start | bytes 2228224 | tf_op jit(solution)/shard_map/all_gather | solution.py:130
  8.2 19.9 %copy-start.16 = (bf16[256,512]{1,0:T(8,128)(2,1)S(1)}, bf16[256,512]{1,0:T(8,128)(2,1)}, u32[]{:S(2)}) copy-start(bf16[256,512]{1,0:T(8,128)(2,1)} %param.10) | copy-start | bytes 786436
  9.3 20.4 %collective-permute-start.1 = (bf16[1,4,64,1024]{3,2,1,0:T(8,128)(2,1)S(1)}, bf16[1,4,64,1024]{3,2,1,0:T(8,128)(2,1)S(1)}, u32[]{:S(2)}, u32[]{:S(2)}) collective-permute-start(bf16[1,4,64,1024]{3,2,1,0:T(8,128)(2,1)S(1)} %bitcast.260), channel_id=1, source_target_pairs={{1,0},{2,1},{3,2},{4,3},{5,4},{6,5},{7,6},{8,7},{9,8},{10,9},{11,1... | collective-permute-start | bytes 1572872 | tf_op jit(solution)/shard_map/ppermute | solution.py:23
  11.2 18.4 %collective-permute-start = (bf16[1,4,64,1024]{3,2,1,0:T(8,128)(2,1)S(1)}, bf16[1,4,64,1024]{3,2,1,0:T(8,128)(2,1)S(1)}, u32[]{:S(2)}, u32[]{:S(2)}) collective-permute-start(bf16[1,4,64,1024]{3,2,1,0:T(8,128)(2,1)S(1)} %bitcast.261), channel_id=1, source_target_pairs={{0,1},{1,2},{2,3},{3,4},{4,5},{5,6},{6,7},{7,8},{8,9},{9,10},{10,1... | collective-permute-start | bytes 1572872 | tf_op jit(solution)/shard_map/ppermute | solution.py:22
  19.6 162.4 %reduce-scatter.2.cloned.1.call-start = ((), (), s32[]{:S(2)}) async-start(), calls=%async_computation.2 | async-start | bytes 4456448 | tf_op jit(solution)/shard_map/reduce_scatter | solution.py:169
  26.4 3.6 %copy-start.6 = (bf16[4,64,8,64]{3,2,1,0:T(8,128)(2,1)}, bf16[4,64,8,64]{3,2,1,0:T(8,128)(2,1)S(1)}, u32[]{:S(2)}) copy-start(bf16[4,64,8,64]{3,2,1,0:T(8,128)(2,1)S(1)} %reshape.185) | copy-start | bytes 786436
  37.9 3.3 %copy-start.1 = (bf16[4,576,512]{1,2,0:T(8,128)(2,1)}, bf16[4,576,512]{1,2,0:T(8,128)(2,1)S(1)}, u32[]{:S(2)}) copy-start(bf16[4,576,512]{1,2,0:T(8,128)(2,1)S(1)} %copy.142) | copy-start | bytes 7077892
  64.3 2.1 %copy-start.13 = (bf16[4,64,8,64]{3,1,0,2:T(8,128)(2,1)S(1)}, bf16[4,64,8,64]{3,1,0,2:T(8,128)(2,1)}, u32[]{:S(2)}) copy-start(bf16[4,64,8,64]{3,1,0,2:T(8,128)(2,1)} %copy.145) | copy-start | bytes 786436
  66.4 2.5 %copy-start = (f32[4,8,576,64]{2,3,1,0:T(8,128)S(1)}, f32[4,8,576,64]{2,3,1,0:T(8,128)}, u32[]{:S(2)}) copy-start(f32[4,8,576,64]{2,3,1,0:T(8,128)} %get-tuple-element.31) | copy-start | bytes 14155780
  68.9 1.4 copy-start.14
  70.2 1.7 copy-start.10
  72.0 2.4 %copy-start.11 = (bf16[4,64,8,64]{1,3,2,0:T(8,128)(2,1)S(1)}, bf16[4,64,8,64]{1,3,2,0:T(8,128)(2,1)}, u32[]{:S(2)}) copy-start(bf16[4,64,8,64]{1,3,2,0:T(8,128)(2,1)} %copy.153) | copy-start | bytes 786436
  74.6 5.1 %copy-start.8 = (bf16[4,64,8,64]{1,3,2,0:T(8,128)(2,1)}, bf16[4,64,8,64]{1,3,2,0:T(8,128)(2,1)S(1)}, u32[]{:S(2)}) copy-start(bf16[4,64,8,64]{1,3,2,0:T(8,128)(2,1)S(1)} %get-tuple-element.5) | copy-start | bytes 786436
  83.6 1.8 copy-start.7
  84.4 1.0 copy-start.5
  85.4 1.1 copy-start.12
  92.3 1.0 copy-start.9
  98.6 1.5 copy-start.4
  144.0 3.8 %copy-start.3 = (f32[4,9,64,512]{3,2,1,0:T(8,128)S(1)}, f32[4,9,64,512]{3,2,1,0:T(8,128)}, u32[]{:S(2)}) copy-start(f32[4,9,64,512]{3,2,1,0:T(8,128)} %concatenate.24) | copy-start | bytes 14155780
  152.4 18.5 %collective-permute-start.3 = (f32[4,64,1024]{2,1,0:T(8,128)}, f32[4,64,1024]{2,1,0:T(8,128)}, u32[]{:S(2)}, u32[]{:S(2)}) collective-permute-start(f32[4,64,1024]{2,1,0:T(8,128)} %slice_bitcast_fusion), channel_id=1, source_target_pairs={{1,0},{2,1},{3,2},{4,3},{5,4},{6,5},{7,6},{8,7},{9,8},{10,9},{11,1... | collective-permute-start | bytes 3145736 | tf_op jit(solution)/shard_map/ppermute | solution.py:31
  156.0 8.7 %copy-start.2 = (bf16[4,576,512]{1,2,0:T(8,128)(2,1)S(1)}, bf16[4,576,512]{1,2,0:T(8,128)(2,1)}, u32[]{:S(2)}) copy-start(bf16[4,576,512]{1,2,0:T(8,128)(2,1)} %copy-done.1) | copy-start | bytes 7077892
  156.0 26.1 %collective-permute-start.2 = (f32[4,64,1024]{2,1,0:T(8,128)}, f32[4,64,1024]{2,1,0:T(8,128)}, u32[]{:S(2)}, u32[]{:S(2)}) collective-permute-start(f32[4,64,1024]{2,1,0:T(8,128)} %slice_bitcast_fusion.4), channel_id=1, source_target_pairs={{0,1},{1,2},{2,3},{3,4},{4,5},{5,6},{6,7},{7,8},{8,9},{9,10},{10,1... | collective-permute-start | bytes 3145736 | tf_op jit(solution)/shard_map/ppermute | solution.py:31
Sparse Core Ops, SparseCore 0:
  19.7 42.2 all-gather.1
  92.5 70.0 reduce-scatter.1
where the time goes:
time: 193 us; the launch traced here: 192 us
  local copies, waits for them, and re-layouts  86.8 us (45%)
  waiting for transfers between devices  32 us (17%)
  matrix products  29.2 us (15%)
  between operations  16.5 us (9%)
  other arithmetic  14.7 us (8%)
  starting transfers between devices  12.6 us (7%)
    dot_general x10, matrix products, product(): return jnp.einsum(form, left, right, preferred_element_type=jnp.float32)  27.3 us
    all_gather x1, waiting for transfers between devices, per_device(): land_panel = lax.all_gather(own_block, 'prow', axis=0, tiled=True)  20.8 us
    concatenate x3, local copies, waits for them, and re-layouts, per_device(): jnp.concatenate([kgrad_win.reshape(PC, 9 * BLK, model_width), vgrad_win.r...  18.5 us
    transpose x2, local copies, waits for them, and re-layouts, product(): return jnp.einsum(form, left, right, preferred_element_type=jnp.float32)  16.7 us
    ppermute x2, waiting for transfers between devices, passed_along(): return lax.ppermute(block, axis, route)  11.1 us
    unnamed x44, local copies, waits for them, and re-layouts  10.4 us
    ppermute x2, starting transfers between devices, passed_along(): return lax.ppermute(block, axis, route)  6.02 us
    reshape x2, local copies, waits for them, and re-layouts, per_device(): vgrad_land.reshape(NLAND, BLK, model_width)  4.89 us
  transfers between devices with their start and end apart: 6, of which 2 were waited for; matrix products, arithmetic and copies ran while one was open for 48% of the time, Pallas kernels for 0%

commit v1 on v0

--- a/solution.py
+++ b/solution.py
@@ -127,7 +127,26 @@
     count_near = lax.dynamic_slice_in_dim(count_padded, my_row, 3, 0)
     own_col = lax.dynamic_index_in_dim(landmark_cols, my_row, 0, keepdims=False)
     own_block = lax.dynamic_slice_in_dim(key_value[0], own_col, 1, 0)
-    land_panel = lax.all_gather(own_block, "prow", axis=0, tiled=True)
+    count, position_2, rows = (lax.axis_size("prow"), lax.axis_index("prow"), own_block.shape[0])
+    forward = [(i_2, (i_2 + 1) % count) for i_2 in range(count)]
+    behind = [(i_2, (i_2 - 1) % count) for i_2 in range(count)]
+    out = jnp.zeros(
+        (*own_block.shape[:0], count * rows, *own_block.shape[0 + 1 :]), own_block.dtype
+    )
+    out = lax.dynamic_update_slice_in_dim(out, own_block, position_2 * rows, axis=0)
+    from_left = from_right = own_block
+    middle_2 = count // 2
+    for turn in range(1, middle_2 + 1):
+        from_left = lax.ppermute(from_left, "prow", forward)
+        out = lax.dynamic_update_slice_in_dim(
+            out, from_left, (position_2 - turn) % count * rows, axis=0
+        )
+        if turn < count - middle_2:
+            from_right = lax.ppermute(from_right, "prow", behind)
+            out = lax.dynamic_update_slice_in_dim(
+                out, from_right, (position_2 + turn) % count * rows, axis=0
+            )
+    land_panel = out
     chosen_rows = landmark_rows[0]
     chosen = jnp.take(land_panel, chosen_rows, axis=0)
     chosen_counts = valid_counts[chosen_rows, landmark_cols[chosen_rows]]

time: 193 us -> 219 us (1.13)
  starting transfers between devices: 12.6 us -> 45.5 us
  waiting for transfers between devices: 32 us -> 7.41 us
  local copies, waits for them, and re-layouts: 86.8 us -> 101 us
    ppermute x0 -> x15, starting transfers between devices: none -> 28.7 us  [the longest x7 23.8 us: per_device(): from_right = lax.ppermute(from_right, 'prow', behind)]
    all_gather x1 -> x0, waiting for transfers between devices: 20.8 us -> none  [per_device(): land_panel = lax.all_gather(own_block, 'prow', axis=0, tiled=True)]
    dynamic_update_slice x0 -> x16, local copies, waits for them, and re-layouts: none -> 12.3 us  [the longest x8 7.06 us: per_device(): lax.dynamic_update_slice_in_dim(out, from_left, (position_2 - turn) % cou...]
    ppermute x2, waiting for transfers between devices: 11.1 us -> 2.06 us  [passed_along(): return lax.ppermute(block, axis, route)]
    ppermute x0 -> x15, waiting for transfers between devices: none -> 5.33 us  [the longest x8 5.31 us: per_device(): from_left = lax.ppermute(from_left, 'prow', forward)]
    ppermute x2, starting transfers between devices: 6.02 us -> 10.3 us  [passed_along(): return lax.ppermute(block, axis, route)]
    slice x2, local copies, waits for them, and re-layouts: 4.48 us -> 6.93 us  [per_device(): values_win = stacked[..., model_width:].reshape(PC, 9 * BLK, HEADS, HD)]
    reduce_sum x1, other arithmetic: 1.37 us -> 3.77 us  [attend(): jnp.sum(jnp.exp(scores_win - row_max[..., None]), axis=-1)]
  transfers between devices with their start and end apart: 6 -> 20, of which waited for: 2 -> 2; matrix products, arithmetic and copies ran while one was open for 48% -> 49% of each run, Pallas kernels for 0% -> 0%
where the time goes in v1:
time: 219 us; the launch traced here: 216 us
  local copies, waits for them, and re-layouts  101 us (46%)
  starting transfers between devices  45.5 us (21%)
  matrix products  29.6 us (14%)
  between operations  16.6 us (8%)
  other arithmetic  15.9 us (7%)
  waiting for transfers between devices  7.41 us (3%)
    dot_general x10, matrix products, product(): return jnp.einsum(form, left, right, preferred_element_type=jnp.float32)  27.8 us
    ppermute x7, starting transfers between devices, per_device(): from_right = lax.ppermute(from_right, 'prow', behind)  23.8 us
    concatenate x3, local copies, waits for them, and re-layouts, per_device(): jnp.concatenate([kgrad_win.reshape(PC, 9 * BLK, model_width), vgrad_win.r...  18.6 us
    transpose x2, local copies, waits for them, and re-layouts, product(): return jnp.einsum(form, left, right, preferred_element_type=jnp.float32)  16.6 us
    ppermute x2, starting transfers between devices, passed_along(): return lax.ppermute(block, axis, route)  10.3 us
    unnamed x62, local copies, waits for them, and re-layouts  9.63 us
    dynamic_update_slice x8, local copies, waits for them, and re-layouts, per_device(): lax.dynamic_update_slice_in_dim(out, from_left, (position_2 - turn) % cou...  7.06 us
    slice x2, local copies, waits for them, and re-layouts, per_device(): values_win = stacked[..., model_width:].reshape(PC, 9 * BLK, HEADS, HD)  6.93 us
  transfers between devices with their start and end apart: 20, of which 2 were waited for; matrix products, arithmetic and copies ran while one was open for 49% of the time, Pallas kernels for 0%

profile of v1, /device:TPU:1, one launch (start us, length us, event | category | flops | bytes accessed | tf_op | source)
XLA Modules:
  0.0 215.8 jit_solution(15527752904727720772)
XLA Ops:
  9.2 2.0 collective-permute-start.1
  11.2 4.5 %collective-permute-start = (bf16[1,4,64,1024]{3,2,1,0:T(8,128)(2,1)S(1)}, bf16[1,4,64,1024]{3,2,1,0:T(8,128)(2,1)S(1)}, u32[]{:S(2)}, u32[]{:S(2)}) collective-permute-start(bf16[1,4,64,1024]{3,2,1,0:T(8,128)(2,1)S(1)} %bitcast.263), channel_id=1, source_target_pairs={{0,1},{1,2},{2,3},{3,4},{4,5},{5,6},{6,7},{7,8},{8,9},{9,10},{10,1... | collective-permute-start | bytes 1572872 | tf_op jit(solution)/shard_map/ppermute | solution.py:22
  15.7 1.2 dynamic_slice.16
  18.9 1.6 broadcast_in_dim.105
  26.0 1.1 reshape.189
  27.1 2.2 %copy.153 = bf16[4,64,8,64]{1,3,2,0:T(8,128)(2,1)} copy(bf16[4,64,8,64]{3,2,1,0:T(8,128)(2,1)} %reshape.189) | data formatting | bytes 524288 | tf_op jit(solution)/shard_map/reshape | solution.py:164
  29.9 2.0 collective-permute-start.4
  32.3 1.6 constant_dynamic-update-slice_fusion.19
  34.6 1.8 collective-permute-start.6
  36.4 3.2 %collective-permute-start.7 = (bf16[1,64,1024]{2,1,0:T(8,128)(2,1)S(1)}, bf16[1,64,1024]{2,1,0:T(8,128)(2,1)S(1)}, u32[]{:S(2)}, u32[]{:S(2)}) collective-permute-start(bf16[1,64,1024]{2,1,0:T(8,128)(2,1)S(1)} %collective-permute-done.5), channel_id=1, source_target_pairs={{0,15},{1,0},{2,1},{3,2},{4,3},{5,4},{6,5},{7,6},{8,7},{9,8},{10,9... | collective-permute-start | bytes 393224 | tf_op jit(solution)/shard_map/ppermute | solution.py:145
  41.5 5.4 %collective-permute-start.9 = (bf16[1,64,1024]{2,1,0:T(8,128)(2,1)S(1)}, bf16[1,64,1024]{2,1,0:T(8,128)(2,1)S(1)}, u32[]{:S(2)}, u32[]{:S(2)}) collective-permute-start(bf16[1,64,1024]{2,1,0:T(8,128)(2,1)S(1)} %collective-permute-done.7), channel_id=1, source_target_pairs={{0,15},{1,0},{2,1},{3,2},{4,3},{5,4},{6,5},{7,6},{8,7},{9,8},{10,9... | collective-permute-start | bytes 393224 | tf_op jit(solution)/shard_map/ppermute | solution.py:145
  46.9 1.6 constant_dynamic-update-slice_fusion.15
  49.8 2.6 %fusion.47 = (bf16[4,576,512]{2,1,0:T(8,128)(2,1)}, bf16[4,576,512]{2,1,0:T(8,128)(2,1)}) fusion(bf16[4,576,1024]{2,1,0:T(8,128)(2,1)S(1)} %bitcast.261), kind=kLoop, calls=%fused_computation.141 | loop fusion | bytes 9437184 | tf_op jit(solution)/shard_map/slice | solution.py:155
  52.4 3.1 %copy.142 = bf16[4,576,512]{1,2,0:T(8,128)(2,1)S(1)} copy(bf16[4,576,512]{2,1,0:T(8,128)(2,1)} %get-tuple-element.18) | data formatting | bytes 4718592 | tf_op jit(solution)/shard_map/slice | solution.py:154
  55.5 3.9 %bitcast_reduce_fusion = (f32[4,8,64]{2,1,0:T(8,128)}, f32[4,8,576,64]{2,3,1,0:T(8,128)}) fusion(pred[4,576]{1,0:T(4,128)(4,1)S(1)} %broadcast_compare_fusion, bf16[4,64,8,64]{1,3,2,0:T(8,128)(2,1)S(1)} %copy.161, bf16[4,576,8,64]{1,3,2,0:T(8,128)(2,1)S(1)} %bitcast.258), kind=kOutput, calls=%fused_computation.8 | convolution fusion | flops 154531840 | bytes 7350528 | tf_op jit(solution)/shard_map/cqhe,cwhe->chqw/dot_general | solution.py:35
  59.5 4.5 %collective-permute-start.11 = (bf16[1,64,1024]{2,1,0:T(8,128)(2,1)S(1)}, bf16[1,64,1024]{2,1,0:T(8,128)(2,1)S(1)}, u32[]{:S(2)}, u32[]{:S(2)}) collective-permute-start(bf16[1,64,1024]{2,1,0:T(8,128)(2,1)S(1)} %collective-permute-done.9), channel_id=1, source_target_pairs={{0,15},{1,0},{2,1},{3,2},{4,3},{5,4},{6,5},{7,6},{8,7},{9,8},{10,9... | collective-permute-start | bytes 393224 | tf_op jit(solution)/shard_map/ppermute | solution.py:145
  64.6 4.3 %copy.132 = bf16[4,576,512]{1,2,0:T(8,128)(2,1)} copy(bf16[4,576,512]{2,1,0:T(8,128)(2,1)} %get-tuple-element.17) | data formatting | bytes 4718592 | tf_op jit(solution)/shard_map/slice | solution.py:155
  69.7 4.4 %collective-permute-start.13 = (bf16[1,64,1024]{2,1,0:T(8,128)(2,1)S(1)}, bf16[1,64,1024]{2,1,0:T(8,128)(2,1)S(1)}, u32[]{:S(2)}, u32[]{:S(2)}) collective-permute-start(bf16[1,64,1024]{2,1,0:T(8,128)(2,1)S(1)} %collective-permute-done.11), channel_id=1, source_target_pairs={{0,15},{1,0},{2,1},{3,2},{4,3},{5,4},{6,5},{7,6},{8,7},{9,8},{10,9... | collective-permute-start | bytes 393224 | tf_op jit(solution)/shard_map/ppermute | solution.py:145
  75.5 5.8 %collective-permute-start.15 = (bf16[1,64,1024]{2,1,0:T(8,128)(2,1)S(1)}, bf16[1,64,1024]{2,1,0:T(8,128)(2,1)S(1)}, u32[]{:S(2)}, u32[]{:S(2)}) collective-permute-start(bf16[1,64,1024]{2,1,0:T(8,128)(2,1)S(1)} %collective-permute-done.13), channel_id=1, source_target_pairs={{0,15},{1,0},{2,1},{3,2},{4,3},{5,4},{6,5},{7,6},{8,7},{9,8},{10,9... | collective-permute-start | bytes 393224 | tf_op jit(solution)/shard_map/ppermute | solution.py:145
  83.9 5.3 %collective-permute-done.16 = bf16[1,64,1024]{2,1,0:T(8,128)(2,1)S(1)} collective-permute-done((bf16[1,64,1024]{2,1,0:T(8,128)(2,1)S(1)}, bf16[1,64,1024]{2,1,0:T(8,128)(2,1)S(1)}, u32[]{:S(2)}, u32[]{:S(2)}) %collective-permute-start.16) | collective-permute-done | bytes 131104 | tf_op jit(solution)/shard_map/ppermute | solution.py:140
  89.8 2.2 %gather_fusion.2 = bf16[4,64,1024]{2,1,0:T(8,128)(2,1)S(1)} fusion(bf16[16,64,1024]{2,1,0:T(8,128)(2,1)} %constant_dynamic-update-slice_fusion.5, s32[1024]{0:T(1024)S(1)} %pad_clamp_fusion), kind=kCustom, calls=%fused_computation.2 | custom fusion | bytes 1048592 | tf_op jit(solution)/shard_map/jit(_take)/gather | solution.py:151
  95.8 3.8 %fusion.1 = f32[4,8,64]{2,1,0:T(8,128)S(1)} fusion(f32[4,8,576,64]{2,3,1,0:T(8,128)} %get-tuple-element.33, f32[4,8,64]{2,1,0:T(8,128)S(1)} %copy_maximum_fusion, pred[4,576]{1,0:T(4,128)(4,1)S(1)} %broadcast_compare_fusion), kind=kLoop, calls=%fused_computation.10 | loop fusion | flops 4716544 | bytes 4737280 | tf_op jit(solution)/shard_map/reduce_sum | solution.py:87
  101.4 2.4 %select_convert_fusion = (bf16[4,64,8,64]{1,3,2,0:T(8,128)(2,1)}, f32[4,64,8,64]{1,3,2,0:T(8,128)S(1)}) fusion(pred[4,64]{1,0:T(4,128)(4,1)S(1)} %copy-done.22, f32[4,64,8,64]{1,3,2,0:T(8,128)S(1)} %convolution_bitcast_fusion.4, bf16[4,576,8,64]{1,3,2,0:T(8,128)(2,1)S(1)} %bitcast.268, f32[4,8,576,64]{2,3,1,0:T(8,128)S(1)} %bitcast.255, ...), kind=kOutput, calls=%fused_computation.63 | convolution fusion | flops 155975680 | bytes 8399360 | tf_op jit(solution)/shard_map/chqw,cwhe->cqhe/dot_general | solution.py:35
  105.1 1.4 convolution_bitcast_fusion.7
  106.5 2.5 %reshape.234 = f32[4,64,512]{1,0,2:T(4,128)} reshape(f32[256,8,64]{0,2,1:T(8,128)} %convolution_bitcast_fusion.7) | data formatting | bytes 1048576 | tf_op jit(solution)/shard_map/reshape | solution.py:182
  109.1 2.4 %copy.179 = f32[4,64,512]{2,1,0:T(8,128)} copy(f32[4,64,512]{1,0,2:T(4,128)} %reshape.234) | data formatting | bytes 1048576 | tf_op jit(solution)/shard_map/reshape | solution.py:182
  111.4 1.4 fusion.51
  115.8 2.5 %broadcast_in_dim.111 = f32[16,64,1024]{2,1,0:T(8,128)} broadcast(f32[]{:T(128)} %constant.145.clone.1), dimensions={} | broadcast | bytes 4194308 | tf_op jit(solution)/shard_map/broadcast_in_dim | solution.py:186
  118.3 3.2 %scatter_fusion = f32[16,64,1024]{2,1,0:T(8,128)} fusion(f32[16,64,1024]{2,1,0:T(8,128)} %broadcast_in_dim.111, s32[4]{0:T(128)S(1)} %fusion.45, f32[4,64,1024]{2,1,0:T(8,128)S(1)} %pad_maximum_fusion), kind=kCustom, calls=%fused_computation.3 | custom fusion | flops 262144 | bytes 3145744 | tf_op jit(solution)/shard_map/scatter-add | solution.py:186
  122.5 5.3 %multiply_convert_fusion = bf16[4,8,64,576]{3,2,1,0:T(8,128)(2,1)S(1)} fusion(f32[4,8,576,64]{2,3,1,0:T(8,128)} %get-tuple-element.33, f32[4,8,64]{2,1,0:T(8,128)S(1)} %bitcast.275, f32[4,8,64]{2,1,0:T(8,128)S(1)} %fusion.35, pred[4,576]{1,0:T(4,128)(4,1)S(1)} %broadcast_compare_fusion, bf16[4,64,8,64]{1,3,2,0:T(8,128)(2,1)S(1)} %copy-done.10, ...), kind=kOutput, calls=%fused_computation.12 | convolution fusion | flops 159252480 | bytes 9718016 | tf_op jit(solution)/shard_map/cqhe,cwhe->chqw/dot_general | solution.py:35
  127.8 1.5 copy-done.5
  129.3 3.1 %convolution_bitcast_fusion = f32[4,576,8,64]{1,3,2,0:T(8,128)} fusion(bf16[4,64,8,64]{1,3,2,0:T(8,128)(2,1)S(1)} %copy.161, bf16[4,8,64,576]{3,2,1,0:T(8,128)(2,1)S(1)} %multiply_convert_fusion), kind=kOutput, calls=%fused_computation.19 | convolution fusion | flops 150994944 | bytes 7340032 | tf_op jit(solution)/shard_map/chqw,cqhe->cwhe/dot_general | solution.py:35
  132.4 8.4 %copy.162 = f32[4,576,8,64]{3,2,1,0:T(8,128)} copy(f32[4,576,8,64]{1,3,2,0:T(8,128)} %convolution_bitcast_fusion) | data formatting | bytes 9437184 | tf_op jit(solution)/shard_map/chqw,cqhe->cwhe/transpose | solution.py:35
  140.8 9.1 %concatenate.23 = f32[4,9,64,512]{3,2,1,0:T(8,128)} reshape(f32[4,576,8,64]{3,2,1,0:T(8,128)} %copy.162) | data formatting | bytes 9437184 | tf_op jit(solution)/shard_map/concatenate | solution.py:173
  150.0 6.1 %convolution_bitcast_fusion.1 = f32[4,576,8,64]{1,3,2,0:T(8,128)} fusion(bf16[4,64,8,64]{1,3,2,0:T(8,128)(2,1)S(1)} %copy-done.10, f32[4,8,576,64]{2,3,1,0:T(8,128)} %get-tuple-element.33, f32[4,8,64]{2,1,0:T(8,128)S(1)} %fusion.35, pred[4,576]{1,0:T(4,128)(4,1)S(1)} %broadcast_compare_fusion), kind=kOutput, calls=%fused_computation.20 | convolution fusion | flops 155713536 | bytes 9709824 | tf_op jit(solution)/shard_map/chqw,cqhe->cwhe/dot_general | solution.py:35
  156.0 8.2 %copy.163 = f32[4,576,8,64]{3,2,1,0:T(8,128)} copy(f32[4,576,8,64]{1,3,2,0:T(8,128)} %convolution_bitcast_fusion.1) | data formatting | bytes 9437184 | tf_op jit(solution)/shard_map/chqw,cqhe->cwhe/transpose | solution.py:35
  164.2 8.9 %concatenate.24 = f32[4,9,64,512]{3,2,1,0:T(8,128)} reshape(f32[4,576,8,64]{3,2,1,0:T(8,128)} %copy.163) | data formatting | bytes 9437184 | tf_op jit(solution)/shard_map/concatenate | solution.py:173
  173.1 3.0 %constant_dynamic-update-slice_fusion.4 = f32[4,9,64,1024]{3,2,1,0:T(8,128)S(1)} fusion(f32[4,9,64,512]{3,2,1,0:T(8,128)} %concatenate.23), kind=kLoop, calls=%fused_computation.88 | loop fusion | bytes 9437184
  177.4 2.9 %slice_bitcast_fusion.11 = (f32[4,64,1024]{2,1,0:T(8,128)}, f32[4,64,1024]{2,1,0:T(8,128)S(1)}, f32[4,64,1024]{2,1,0:T(8,128)S(1)}, f32[4,64,1024]{2,1,0:T(8,128...) fusion(f32[4,9,64,1024]{3,2,1,0:T(8,128)S(1)} %constant_dynamic, ...), kind=kLoop, calls=%fused_computation.59 | loop fusion | bytes 18874368 | tf_op jit(solution)/shard_map/squeeze | solution.py:63
  180.6 1.1 slice_bitcast_fusion
  181.7 8.1 %collective-permute-start.18 = (f32[4,64,1024]{2,1,0:T(8,128)}, f32[4,64,1024]{2,1,0:T(8,128)}, u32[]{:S(2)}, u32[]{:S(2)}) collective-permute-start(f32[4,64,1024]{2,1,0:T(8,128)} %slice_bitcast_fusion), channel_id=1, source_target_pairs={{1,0},{2,1},{3,2},{4,3},{5,4},{6,5},{7,6},{8,7},{9,8},{10,9},{11,1... | collective-permute-start | bytes 3145736 | tf_op jit(solution)/shard_map/ppermute | solution.py:31
  191.1 2.2 %collective-permute-start.17 = (f32[4,64,1024]{2,1,0:T(8,128)}, f32[4,64,1024]{2,1,0:T(8,128)}, u32[]{:S(2)}, u32[]{:S(2)}) collective-permute-start(f32[4,64,1024]{2,1,0:T(8,128)} %slice_bitcast_fusion.4), channel_id=1, source_target_pairs={{0,1},{1,2},{2,3},{3,4},{4,5},{5,6},{6,7},{7,8},{8,9},{9,10},{10,1... | collective-permute-start | bytes 3145736 | tf_op jit(solution)/shard_map/ppermute | solution.py:31
  193.9 1.4 copy.152
  196.3 1.8 convolution_bitcast_fusion.2
  198.2 2.8 %fusion.16 = bf16[4,64,8,64]{1,3,2,0:T(8,128)(2,1)S(1)} fusion(f32[4,64,8,64]{1,3,2,0:T(8,128)S(1)} %convolution_bitcast_fusion.2, bf16[4,576,8,64]{1,3,2,0:T(8,128)(2,1)S(1)} %bitcast.259, bf16[4,8,64,576]{3,2,1,0:T(8,128)(2,1)} %copy-done.5), kind=kOutput, calls=%fused_computation.41 | convolution fusion | flops 151257088 | bytes 5505024 | tf_op jit(solution)/shard_map/chqw,cwhe->cqhe/dot_general | solution.py:35
  202.3 1.8 add_bitcast_fusion.2
  204.1 2.1 collective-permute-done.17
  206.2 2.0 fusion.20
  (158 shorter events, 35.9 us)
Async XLA Ops:
  7.2 14.5 %copy-start.23 = (s32[1,4]{1,0:T(1,128)S(1)}, s32[1,4]{1,0:T(1,128)}, u32[]{:S(2)}) copy-start(s32[1,4]{1,0:T(1,128)} %param.13) | copy-start | bytes 52
  7.2 15.0 %copy-start.18 = (bf16[256,512]{1,0:T(8,128)(2,1)S(1)}, bf16[256,512]{1,0:T(8,128)(2,1)}, u32[]{:S(2)}) copy-start(bf16[256,512]{1,0:T(8,128)(2,1)} %param.7) | copy-start | bytes 786436
  7.2 199.0 %reduce-scatter.2.cloned.1.call-start = ((), (), s32[]{:S(2)}) async-start(), calls=%async_computation.1 | async-start | bytes 4456448 | tf_op jit(solution)/shard_map/reduce_scatter | solution.py:188
  9.2 39.9 %collective-permute-start.1 = (bf16[1,4,64,1024]{3,2,1,0:T(8,128)(2,1)S(1)}, bf16[1,4,64,1024]{3,2,1,0:T(8,128)(2,1)S(1)}, u32[]{:S(2)}, u32[]{:S(2)}) collective-permute-start(bf16[1,4,64,1024]{3,2,1,0:T(8,128)(2,1)S(1)} %bitcast.262), channel_id=1, source_target_pairs={{1,0},{2,1},{3,2},{4,3},{5,4},{6,5},{7,6},{8,7},{9,8},{10,9},{11,1... | collective-permute-start | bytes 1572872 | tf_op jit(solution)/shard_map/ppermute | solution.py:23
  11.2 37.9 %collective-permute-start = (bf16[1,4,64,1024]{3,2,1,0:T(8,128)(2,1)S(1)}, bf16[1,4,64,1024]{3,2,1,0:T(8,128)(2,1)S(1)}, u32[]{:S(2)}, u32[]{:S(2)}) collective-permute-start(bf16[1,4,64,1024]{3,2,1,0:T(8,128)(2,1)S(1)} %bitcast.263), channel_id=1, source_target_pairs={{0,1},{1,2},{2,3},{3,4},{4,5},{5,6},{6,7},{7,8},{8,9},{9,10},{10,1... | collective-permute-start | bytes 1572872 | tf_op jit(solution)/shard_map/ppermute | solution.py:22
  20.5 3.4 %copy-start.1 = (s32[16,4]{0,1:T(4,128)S(1)}, s32[16,4]{0,1:T(4,128)}, u32[]{:S(2)}) copy-start(s32[16,4]{0,1:T(4,128)} %param.11) | copy-start | bytes 772
  20.5 3.6 %copy-start = (s32[16]{0:T(128)S(1)}, s32[16]{0:T(128)}, u32[]{:S(2)}) copy-start(s32[16]{0:T(128)} %param.12) | copy-start | bytes 196
  21.2 4.8 %copy-start.19 = (bf16[256,512]{1,0:T(8,128)(2,1)S(1)}, bf16[256,512]{1,0:T(8,128)(2,1)}, u32[]{:S(2)}) copy-start(bf16[256,512]{1,0:T(8,128)(2,1)} %param.10) | copy-start | bytes 786436
  21.2 8.7 %collective-permute-start.2 = (bf16[1,64,1024]{2,1,0:T(8,128)(2,1)S(1)}, bf16[1,64,1024]{2,1,0:T(8,128)(2,1)}, u32[]{:S(2)}, u32[]{:S(2)}) collective-permute-start(bf16[1,64,1024]{2,1,0:T(8,128)(2,1)S(1)} %get-tuple-element.7), channel_id=1, source_target_pairs={{0,1},{1,2},{2,3},{3,4},{4,5},{5,6},{6,7},{7,8},{8,9},{9,10},{10,1... | collective-permute-start | bytes 393224 | tf_op jit(solution)/shard_map/ppermute | solution.py:140
  21.7 10.1 %collective-permute-start.3 = (bf16[1,64,1024]{2,1,0:T(8,128)(2,1)S(1)}, bf16[1,64,1024]{2,1,0:T(8,128)(2,1)S(1)}, u32[]{:S(2)}, u32[]{:S(2)}) collective-permute-start(bf16[1,64,1024]{2,1,0:T(8,128)(2,1)S(1)} %get-tuple-element.7), channel_id=1, source_target_pairs={{0,15},{1,0},{2,1},{3,2},{4,3},{5,4},{6,5},{7,6},{8,7},{9,8},{10,9... | collective-permute-start | bytes 393224 | tf_op jit(solution)/shard_map/ppermute | solution.py:145
  22.5 6.8 %copy-start.7 = (bf16[4,64,8,64]{3,2,1,0:T(8,128)(2,1)}, bf16[4,64,8,64]{3,2,1,0:T(8,128)(2,1)S(1)}, u32[]{:S(2)}) copy-start(bf16[4,64,8,64]{3,2,1,0:T(8,128)(2,1)S(1)} %reshape.185) | copy-start | bytes 786436
  29.9 4.7 %collective-permute-start.4 = (bf16[1,64,1024]{2,1,0:T(8,128)(2,1)}, bf16[1,64,1024]{2,1,0:T(8,128)(2,1)S(1)}, u32[]{:S(2)}, u32[]{:S(2)}) collective-permute-start(bf16[1,64,1024]{2,1,0:T(8,128)(2,1)} %collective-permute-done.2), channel_id=1, source_target_pairs={{0,1},{1,2},{2,3},{3,4},{4,5},{5,6},{6,7},{7,8},{8,9},{9,10},{10,1... | collective-permute-start | bytes 393224 | tf_op jit(solution)/shard_map/ppermute | solution.py:140
  31.8 4.6 %collective-permute-start.5 = (bf16[1,64,1024]{2,1,0:T(8,128)(2,1)S(1)}, bf16[1,64,1024]{2,1,0:T(8,128)(2,1)S(1)}, u32[]{:S(2)}, u32[]{:S(2)}) collective-permute-start(bf16[1,64,1024]{2,1,0:T(8,128)(2,1)S(1)} %collective-permute-done.3), channel_id=1, source_target_pairs={{0,15},{1,0},{2,1},{3,2},{4,3},{5,4},{6,5},{7,6},{8,7},{9,8},{10,9... | collective-permute-start | bytes 393224 | tf_op jit(solution)/shard_map/ppermute | solution.py:145
  34.6 6.3 %collective-permute-start.6 = (bf16[1,64,1024]{2,1,0:T(8,128)(2,1)S(1)}, bf16[1,64,1024]{2,1,0:T(8,128)(2,1)}, u32[]{:S(2)}, u32[]{:S(2)}) collective-permute-start(bf16[1,64,1024]{2,1,0:T(8,128)(2,1)S(1)} %collective-permute-done.4), channel_id=1, source_target_pairs={{0,1},{1,2},{2,3},{3,4},{4,5},{5,6},{6,7},{7,8},{8,9},{9,10},{10,1... | collective-permute-start | bytes 393224 | tf_op jit(solution)/shard_map/ppermute | solution.py:140
  36.4 5.0 %collective-permute-start.7 = (bf16[1,64,1024]{2,1,0:T(8,128)(2,1)S(1)}, bf16[1,64,1024]{2,1,0:T(8,128)(2,1)S(1)}, u32[]{:S(2)}, u32[]{:S(2)}) collective-permute-start(bf16[1,64,1024]{2,1,0:T(8,128)(2,1)S(1)} %collective-permute-done.5), channel_id=1, source_target_pairs={{0,15},{1,0},{2,1},{3,2},{4,3},{5,4},{6,5},{7,6},{8,7},{9,8},{10,9... | collective-permute-start | bytes 393224 | tf_op jit(solution)/shard_map/ppermute | solution.py:145
  40.9 18.5 %collective-permute-start.8 = (bf16[1,64,1024]{2,1,0:T(8,128)(2,1)}, bf16[1,64,1024]{2,1,0:T(8,128)(2,1)S(1)}, u32[]{:S(2)}, u32[]{:S(2)}) collective-permute-start(bf16[1,64,1024]{2,1,0:T(8,128)(2,1)} %collective-permute-done.6), channel_id=1, source_target_pairs={{0,1},{1,2},{2,3},{3,4},{4,5},{5,6},{6,7},{7,8},{8,9},{9,10},{10,1... | collective-permute-start | bytes 393224 | tf_op jit(solution)/shard_map/ppermute | solution.py:140
  41.5 18.0 %collective-permute-start.9 = (bf16[1,64,1024]{2,1,0:T(8,128)(2,1)S(1)}, bf16[1,64,1024]{2,1,0:T(8,128)(2,1)S(1)}, u32[]{:S(2)}, u32[]{:S(2)}) collective-permute-start(bf16[1,64,1024]{2,1,0:T(8,128)(2,1)S(1)} %collective-permute-done.7), channel_id=1, source_target_pairs={{0,15},{1,0},{2,1},{3,2},{4,3},{5,4},{6,5},{7,6},{8,7},{9,8},{10,9... | collective-permute-start | bytes 393224 | tf_op jit(solution)/shard_map/ppermute | solution.py:145
  55.5 3.9 %copy-start.2 = (bf16[4,576,512]{1,2,0:T(8,128)(2,1)}, bf16[4,576,512]{1,2,0:T(8,128)(2,1)S(1)}, u32[]{:S(2)}) copy-start(bf16[4,576,512]{1,2,0:T(8,128)(2,1)S(1)} %copy.142) | copy-start | bytes 7077892
  59.5 10.2 %collective-permute-start.10 = (bf16[1,64,1024]{2,1,0:T(8,128)(2,1)S(1)}, bf16[1,64,1024]{2,1,0:T(8,128)(2,1)S(1)}, u32[]{:S(2)}, u32[]{:S(2)}) collective-permute-start(bf16[1,64,1024]{2,1,0:T(8,128)(2,1)S(1)} %collective-permute-done.8), channel_id=1, source_target_pairs={{0,1},{1,2},{2,3},{3,4},{4,5},{5,6},{6,7},{7,8},{8,9},{9,10},{10,1... | collective-permute-start | bytes 393224 | tf_op jit(solution)/shard_map/ppermute | solution.py:140
  59.5 10.2 %collective-permute-start.11 = (bf16[1,64,1024]{2,1,0:T(8,128)(2,1)S(1)}, bf16[1,64,1024]{2,1,0:T(8,128)(2,1)S(1)}, u32[]{:S(2)}, u32[]{:S(2)}) collective-permute-start(bf16[1,64,1024]{2,1,0:T(8,128)(2,1)S(1)} %collective-permute-done.9), channel_id=1, source_target_pairs={{0,15},{1,0},{2,1},{3,2},{4,3},{5,4},{6,5},{7,6},{8,7},{9,8},{10,9... | collective-permute-start | bytes 393224 | tf_op jit(solution)/shard_map/ppermute | solution.py:145
  69.0 23.0 %copy-start.21 = (pred[4]{0:T(512)(128)(4,1)S(1)}, pred[4]{0:T(512)(128)(4,1)}, u32[]{:S(2)}) copy-start(pred[4]{0:T(512)(128)(4,1)} %compare_and_fusion) | copy-start | bytes 16
  69.6 5.8 %collective-permute-start.12 = (bf16[1,64,1024]{2,1,0:T(8,128)(2,1)S(1)}, bf16[1,64,1024]{2,1,0:T(8,128)(2,1)S(1)}, u32[]{:S(2)}, u32[]{:S(2)}) collective-permute-start(bf16[1,64,1024]{2,1,0:T(8,128)(2,1)S(1)} %collective-permute-done.10), channel_id=1, source_target_pairs={{0,1},{1,2},{2,3},{3,4},{4,5},{5,6},{6,7},{7,8},{8,9},{9,10},{10,1... | collective-permute-start | bytes 393224 | tf_op jit(solution)/shard_map/ppermute | solution.py:140
  69.7 5.8 %collective-permute-start.13 = (bf16[1,64,1024]{2,1,0:T(8,128)(2,1)S(1)}, bf16[1,64,1024]{2,1,0:T(8,128)(2,1)S(1)}, u32[]{:S(2)}, u32[]{:S(2)}) collective-permute-start(bf16[1,64,1024]{2,1,0:T(8,128)(2,1)S(1)} %collective-permute-done.11), channel_id=1, source_target_pairs={{0,15},{1,0},{2,1},{3,2},{4,3},{5,4},{6,5},{7,6},{8,7},{9,8},{10,9... | collective-permute-start | bytes 393224 | tf_op jit(solution)/shard_map/ppermute | solution.py:145
  75.4 7.1 %collective-permute-start.14 = (bf16[1,64,1024]{2,1,0:T(8,128)(2,1)S(1)}, bf16[1,64,1024]{2,1,0:T(8,128)(2,1)S(1)}, u32[]{:S(2)}, u32[]{:S(2)}) collective-permute-start(bf16[1,64,1024]{2,1,0:T(8,128)(2,1)S(1)} %collective-permute-done.12), channel_id=1, source_target_pairs={{0,1},{1,2},{2,3},{3,4},{4,5},{5,6},{6,7},{7,8},{8,9},{9,10},{10,1... | collective-permute-start | bytes 393224 | tf_op jit(solution)/shard_map/ppermute | solution.py:140
  75.5 7.7 %collective-permute-start.15 = (bf16[1,64,1024]{2,1,0:T(8,128)(2,1)S(1)}, bf16[1,64,1024]{2,1,0:T(8,128)(2,1)S(1)}, u32[]{:S(2)}, u32[]{:S(2)}) collective-permute-start(bf16[1,64,1024]{2,1,0:T(8,128)(2,1)S(1)} %collective-permute-done.13), channel_id=1, source_target_pairs={{0,15},{1,0},{2,1},{3,2},{4,3},{5,4},{6,5},{7,6},{8,7},{9,8},{10,9... | collective-permute-start | bytes 393224 | tf_op jit(solution)/shard_map/ppermute | solution.py:145
  82.5 6.6 %collective-permute-start.16 = (bf16[1,64,1024]{2,1,0:T(8,128)(2,1)S(1)}, bf16[1,64,1024]{2,1,0:T(8,128)(2,1)S(1)}, u32[]{:S(2)}, u32[]{:S(2)}) collective-permute-start(bf16[1,64,1024]{2,1,0:T(8,128)(2,1)S(1)} %collective-permute-done.14), channel_id=1, source_target_pairs={{0,1},{1,2},{2,3},{3,4},{4,5},{5,6},{6,7},{7,8},{8,9},{9,10},{10,1... | collective-permute-start | bytes 393224 | tf_op jit(solution)/shard_map/ppermute | solution.py:140
  92.1 2.0 copy-start.15
  94.1 0.8 copy-start.20
  94.9 5.5 %slice-start = ((s8[5242880]{0:T(1024)(128)(4,1)}), s8[4194304]{0:T(1024)(128)(4,1)S(1)}, s32[]{:S(2)}) async-start(s8[5242880]{0:T(1024)(128)(4,1)} %bitcast.254), calls=%async_computation.2 | async-start | bytes 8388608
  95.8 3.9 %copy-start.17 = (bf16[256,8,64]{0,2,1:T(8,128)(2,1)S(1)}, bf16[256,8,64]{0,2,1:T(8,128)(2,1)}, u32[]{:S(2)}) copy-start(bf16[256,8,64]{0,2,1:T(8,128)(2,1)} %copy.150) | copy-start | bytes 786436
  95.8 4.6 %slice-start.1 = ((s8[5242880]{0:T(1024)(128)(4,1)}), s8[1048576]{0:T(1024)(128)(4,1)S(1)}, s32[]{:S(2)}) async-start(s8[5242880]{0:T(1024)(128)(4,1)} %bitcast.254), calls=%async_computation.3 | async-start | bytes 2097152
  99.6 1.7 copy-start.12
  99.6 1.7 copy-start.22
  101.4 2.4 %copy-start.13 = (bf16[4,64,8,64]{1,3,2,0:T(8,128)(2,1)S(1)}, bf16[4,64,8,64]{1,3,2,0:T(8,128)(2,1)}, u32[]{:S(2)}) copy-start(bf16[4,64,8,64]{1,3,2,0:T(8,128)(2,1)} %copy.153) | copy-start | bytes 786436
  104.0 2.5 %copy-start.9 = (bf16[4,64,8,64]{1,3,2,0:T(8,128)(2,1)}, bf16[4,64,8,64]{1,3,2,0:T(8,128)(2,1)S(1)}, u32[]{:S(2)}) copy-start(bf16[4,64,8,64]{1,3,2,0:T(8,128)(2,1)S(1)} %get-tuple-element.5) | copy-start | bytes 786436
  106.5 4.9 %copy-start.16 = (bf16[4,64,8,64]{3,1,0,2:T(8,128)(2,1)S(1)}, bf16[4,64,8,64]{3,1,0,2:T(8,128)(2,1)}, u32[]{:S(2)}) copy-start(bf16[4,64,8,64]{3,1,0,2:T(8,128)(2,1)} %copy.156) | copy-start | bytes 786436
  112.8 1.8 copy-start.8
  113.6 1.0 copy-start.6
  114.6 1.1 copy-start.14
  121.5 1.0 copy-start.10
  127.8 1.5 copy-start.5
  173.1 3.8 %copy-start.4 = (f32[4,9,64,512]{3,2,1,0:T(8,128)S(1)}, f32[4,9,64,512]{3,2,1,0:T(8,128)}, u32[]{:S(2)}) copy-start(f32[4,9,64,512]{3,2,1,0:T(8,128)} %concatenate.24) | copy-start | bytes 14155780
  181.7 22.4 %collective-permute-start.18 = (f32[4,64,1024]{2,1,0:T(8,128)}, f32[4,64,1024]{2,1,0:T(8,128)}, u32[]{:S(2)}, u32[]{:S(2)}) collective-permute-start(f32[4,64,1024]{2,1,0:T(8,128)} %slice_bitcast_fusion), channel_id=1, source_target_pairs={{1,0},{2,1},{3,2},{4,3},{5,4},{6,5},{7,6},{8,7},{9,8},{10,9},{11,1... | collective-permute-start | bytes 3145736 | tf_op jit(solution)/shard_map/ppermute | solution.py:31
  191.1 7.1 %copy-start.3 = (bf16[4,576,512]{1,2,0:T(8,128)(2,1)S(1)}, bf16[4,576,512]{1,2,0:T(8,128)(2,1)}, u32[]{:S(2)}) copy-start(bf16[4,576,512]{1,2,0:T(8,128)(2,1)} %copy-done.2) | copy-start | bytes 7077892
  191.1 15.1 %collective-permute-start.17 = (f32[4,64,1024]{2,1,0:T(8,128)}, f32[4,64,1024]{2,1,0:T(8,128)}, u32[]{:S(2)}, u32[]{:S(2)}) collective-permute-start(f32[4,64,1024]{2,1,0:T(8,128)} %slice_bitcast_fusion.4), channel_id=1, source_target_pairs={{0,1},{1,2},{2,3},{3,4},{4,5},{5,6},{6,7},{7,8},{8,9},{9,10},{10,1... | collective-permute-start | bytes 3145736 | tf_op jit(solution)/shard_map/ppermute | solution.py:31
  200.9 1.4 copy-start.11
Sparse Core Ops, SparseCore 0:
  121.6 80.0 reduce-scatter.1
